TPU v7x, 32 devices: a whole 2x2x4 slice. The times are simulated.
32 devices in a mesh: dp: 8 (over y, x, core), tensor: 4 (over z).
Axes of the slice: x: 2, y: 2, z: 4, core: 2. Of those that a mesh axis runs over, the one named last changes fastest.
Arguments:
- tokens: bfloat16 [8192, 2048], P(('dp', 'tensor')), may hold values from -6 to 6
- cotangent: bfloat16 [8192, 2048], P(('dp', 'tensor')), may hold values from -6 to 6
- norm_gains: float32 [2, 2048], replicated, may hold values from 0.1 to 1.9
- norm_shifts: float32 [2, 2048], replicated, may hold values from -4 to 4
- query_key_value_weight: bfloat16 [2048, 3, 2048], P(None, None, 'tensor'), may hold values from -0.125 to 0.125
- b_qv: float32 [2, 2048], P(None, 'tensor'), may hold values from -4 to 4
- output_weight: bfloat16 [2048, 2048], P('tensor'), may hold values from -0.375 to 0.375
- output_bias_vector: float32 [2048], replicated, may hold values from -4 to 4
- up_weight: bfloat16 [2048, 8192], P(None, 'tensor'), may hold values from -0.125 to 0.125
- b_up: float32 [8192], P('tensor'), may hold values from -4 to 4
- down_weight: bfloat16 [8192, 2048], P('tensor'), may hold values from -0.0625 to 0.0625
- down_bias_vector: float32 [2048], replicated, may hold values from -4 to 4
- adapter_query_key_value_input: bfloat16 [8, 16, 2048], replicated, may hold values from -0.125 to 0.125
- qkv_out: bfloat16 [8, 16, 3, 2048], P(None, None, None, 'tensor'), may hold values from -1.5 to 1.5
- adapter_output_input: bfloat16 [8, 16, 2048], P(None, None, 'tensor'), may hold values from -0.375 to 0.375
- adapter_output_output: bfloat16 [8, 16, 2048], replicated, may hold values from -1.5 to 1.5
- adapter_up_input: bfloat16 [8, 16, 2048], replicated, may hold values from -0.125 to 0.125
- up_out: bfloat16 [8, 16, 8192], P(None, None, 'tensor'), may hold values from -1.5 to 1.5
- down_in: bfloat16 [8, 16, 8192], P(None, None, 'tensor'), may hold values from -0.0625 to 0.0625
- adapter_down_output: bfloat16 [8, 16, 2048], replicated, may hold values from -1.5 to 1.5
- offsets: int32 [8, 2], P('dp'), may hold values from 0 to 768, as said below
- adapter_ids: int32 [8, 4], P('dp'), may hold values from 0 to 7
Outputs:
- out: bfloat16 [8192, 2048], P(('dp', 'tensor'))
- in_grad: bfloat16 [8192, 2048], P(('dp', 'tensor'))
- g_qkv_in: float32 [8, 16, 2048], replicated
- g_qkv_out: float32 [8, 16, 3, 2048], P(None, None, None, 'tensor')
- g_out_in: float32 [8, 16, 2048], P(None, None, 'tensor')
- g_out_out: float32 [8, 16, 2048], replicated
- g_up_in: float32 [8, 16, 2048], replicated
- g_up_out: float32 [8, 16, 8192], P(None, None, 'tensor')
- g_down_in: float32 [8, 16, 8192], P(None, None, 'tensor')
- g_down_out: float32 [8, 16, 2048], replicated
Inputs may be any that keep to these rules, and one draw needn't show every extreme that they name: For every sequence s, offsets[s, 0] + 256 <= offsets[s, 1]: the two pieces of 256 positions lie inside the sequence and don't intersect.
All inputs are finite; a program needn't handle non-finite values.
Results may differ from a plain program's by a relative error of at most 0.02.
Values may be sent and summed in bfloat16 or wider, within the bound.
A program may use at most 192 MiB of HBM per device.

v0:
```python
import math
import jax
import jax.numpy as jnp
from jax import lax
from jax.sharding import PartitionSpec as P

HEADS = 16
HEAD_DIM = 128
PIECE = 256
EPS = 1e-05
GELU_C = 0.7978845608028654
GELU_K = 0.044715
NEGATIVE = -1e30
EXACT_MODE = lax.Precision.HIGHEST


def layer_norm(values, gain_row, shift_row):
    centre = values - jnp.mean(values, axis=-1, keepdims=True)
    spread = jnp.mean(centre * centre, axis=-1, keepdims=True)
    inverse = lax.rsqrt(spread + EPS)
    scaled = centre * inverse
    return (scaled * gain_row + shift_row, scaled, inverse)


def norm_back(grad_rows, scaled, inverse, gain_row):
    inner_grad = grad_rows * gain_row
    first_mean = jnp.mean(inner_grad, axis=-1, keepdims=True)
    second_mean = jnp.mean(inner_grad * scaled, axis=-1, keepdims=True)
    return inverse * (inner_grad - first_mean - scaled * second_mean)


def gelu_parts(values):
    cubic = GELU_K * values * values * values
    tangent = jnp.tanh(GELU_C * (values + cubic))
    gelu_value = 0.5 * values * (1.0 + tangent)
    gelu_slope = 0.5 * (1.0 + tangent) + 0.5 * values * (1.0 - tangent * tangent) * GELU_C * (
        1.0 + 3.0 * GELU_K * values * values
    )
    return (gelu_value, gelu_slope)


def dot_transposed(left, right):
    return lax.dot_general(
        left, right, (((1,), (1,)), ((), ())), preferred_element_type=jnp.float32
    )


def choose(adapter_table, indicator_matrix):
    picked = jnp.einsum(
        "ge,erm->grm", indicator_matrix, adapter_table, preferred_element_type=jnp.float32
    )
    return picked.astype(jnp.bfloat16)


def low_rank_down(activations, chosen):
    shaped = activations.reshape(chosen.shape[0], -1, activations.shape[-1])
    return jnp.einsum("glm,grm->glr", shaped, chosen, preferred_element_type=jnp.float32)


def low_rank_upward(rank_rows, chosen):
    product = jnp.einsum(
        "glr,grm->glm", rank_rows, chosen.astype(jnp.float32), precision=EXACT_MODE
    )
    return product.reshape(-1, product.shape[-1])


def rank_grad(rank_rows, activations):
    shaped = activations.reshape(rank_rows.shape[0], -1, activations.shape[-1]).astype(jnp.float32)
    return jnp.einsum("glr,glm->grm", rank_rows, shaped, precision=EXACT_MODE)


def to_tables(per_sequence, indicator_matrix):
    return jnp.einsum("ge,grm->erm", indicator_matrix, per_sequence, precision=EXACT_MODE)


def block_scores(query_rows, key_rows, pieces, slopes, first_row):
    rows_here = query_rows.shape[1]
    length = key_rows.shape[1]
    keys_at = jnp.arange(length, dtype=jnp.int32)
    query_at = first_row + jnp.arange(rows_here, dtype=jnp.int32)
    scaling = 1.0 / math.sqrt(key_rows.shape[3])
    scores = (
        jnp.einsum("gqhd,gkhd->ghqk", query_rows, key_rows, preferred_element_type=jnp.float32)
        * scaling
    )
    distance = jnp.abs(query_at[:, None] - keys_at[None, :]).astype(jnp.float32)
    scores = scores - slopes[None, :, None, None] * distance[None, None]
    piece_rows = pieces[:, first_row : first_row + rows_here]
    allowed = (keys_at[None, None, :] <= query_at[None, :, None]) | (
        piece_rows[:, :, None] == pieces[:, None, :]
    ) & (piece_rows[:, :, None] > 0)
    return jnp.where(allowed[:, None], scores, NEGATIVE)


def attend(queries, key_rows, values, pieces, slopes):
    length = queries.shape[1]
    block_rows = min(512, length)
    contexts = []
    log_sums = []
    for first_row in range(0, length, block_rows):
        scores = block_scores(
            queries[:, first_row : first_row + block_rows], key_rows, pieces, slopes, first_row
        )
        row_peak = jnp.max(scores, axis=-1, keepdims=True)
        exponent = jnp.exp(scores - row_peak)
        total_sum = jnp.sum(exponent, axis=-1, keepdims=True)
        weights = (exponent / total_sum).astype(jnp.bfloat16)
        contexts.append(
            jnp.einsum("ghqk,gkhd->gqhd", weights, values, preferred_element_type=jnp.float32)
        )
        log_sums.append(row_peak + jnp.log(total_sum))
    return (jnp.concatenate(contexts, 1), jnp.concatenate(log_sums, 2))


def attend_back(queries, key_rows, values, pieces, slopes, log_sums, grad_context):
    length = queries.shape[1]
    block_rows = min(512, length)
    scaling = 1.0 / math.sqrt(key_rows.shape[3])
    grad_queries = []
    grad_keys = jnp.zeros(key_rows.shape, jnp.float32)
    grad_values = jnp.zeros(values.shape, jnp.float32)
    for first_row in range(0, length, block_rows):
        query_rows = queries[:, first_row : first_row + block_rows]
        grad_rows = grad_context[:, first_row : first_row + block_rows]
        scores = block_scores(query_rows, key_rows, pieces, slopes, first_row)
        probability = jnp.exp(scores - log_sums[:, :, first_row : first_row + block_rows])
        grad_values = grad_values + jnp.einsum(
            "ghqk,gqhd->gkhd",
            probability.astype(jnp.bfloat16),
            grad_rows,
            preferred_element_type=jnp.float32,
        )
        grad_probs = jnp.einsum(
            "gqhd,gkhd->ghqk", grad_rows, values, preferred_element_type=jnp.float32
        )
        inner_sum = jnp.sum(probability * grad_probs, axis=-1, keepdims=True)
        grad_scores = (probability * (grad_probs - inner_sum)).astype(jnp.bfloat16)
        grad_queries.append(
            jnp.einsum("ghqk,gkhd->gqhd", grad_scores, key_rows, preferred_element_type=jnp.float32)
            * scaling
        )
        grad_keys = (
            grad_keys
            + jnp.einsum(
                "ghqk,gqhd->gkhd", grad_scores, query_rows, preferred_element_type=jnp.float32
            )
            * scaling
        )
    return (jnp.concatenate(grad_queries, 1), grad_keys, grad_values)


def body(
    tokens,
    cotangent,
    norm_gains,
    norm_shifts,
    query_key_value_weight,
    b_qv,
    output_weight,
    output_bias_vector,
    up_weight,
    b_up,
    down_weight,
    down_bias_vector,
    adapter_query_key_value_input,
    qkv_out,
    adapter_output_input,
    adapter_output_output,
    adapter_up_input,
    up_out,
    down_in,
    adapter_down_output,
    offsets,
    adapter_ids,
):
    row_count = tokens.shape[0]
    model_width = tokens.shape[1]
    position = lax.axis_index("tensor")
    seq_count = offsets.shape[0]
    full_rows = row_count * lax.axis_size("tensor")
    length = full_rows // seq_count
    local_width = query_key_value_weight.shape[2]
    local_heads = local_width // HEAD_DIM
    table_count = adapter_query_key_value_input.shape[0]
    indicator_matrix = (
        adapter_ids[:, :, None] == jnp.arange(table_count, dtype=jnp.int32)[None, None, :]
    ).astype(jnp.float32)
    one_low = indicator_matrix.astype(jnp.bfloat16)
    chosen_qkv_in = choose(adapter_query_key_value_input, one_low[:, 0])
    chosen_qkv_out = choose(
        qkv_out.reshape(table_count, qkv_out.shape[1], 3 * local_width), one_low[:, 0]
    )
    chosen_out_in = choose(adapter_output_input, one_low[:, 1])
    chosen_out_out = choose(adapter_output_output, one_low[:, 1])
    chosen_up_in = choose(adapter_up_input, one_low[:, 2])
    chosen_up_out = choose(up_out, one_low[:, 2])
    chosen_down_in = choose(down_in, one_low[:, 3])
    chosen_down_out = choose(adapter_down_output, one_low[:, 3])
    where_at = jnp.arange(length, dtype=jnp.int32)
    first_piece = (
        (where_at[None, :] >= offsets[:, 0:1]) & (where_at[None, :] < offsets[:, 0:1] + PIECE)
    ).astype(jnp.int32)
    second_piece = (
        (where_at[None, :] >= offsets[:, 1:2]) & (where_at[None, :] < offsets[:, 1:2] + PIECE)
    ).astype(jnp.int32)
    pieces = first_piece + 2 * second_piece
    head_ids = (position * local_heads + jnp.arange(local_heads, dtype=jnp.int32)).astype(
        jnp.float32
    )
    slopes = jnp.exp2(-8.0 * (head_ids + 1.0) / HEADS)
    qkv_flat = query_key_value_weight.reshape(model_width, 3 * local_width)
    qkv_bias = jnp.concatenate([b_qv[0], jnp.zeros_like(b_qv[0]), b_qv[1]])
    inputs = tokens.astype(jnp.float32)
    normed_local, scaled_first, inverse_first = layer_norm(inputs, norm_gains[0], norm_shifts[0])
    sent_in = normed_local.astype(jnp.bfloat16)
    arrived = lax.all_gather(sent_in, "tensor", axis=0, tiled=True)
    low_rank_query_key_value = low_rank_down(arrived, chosen_qkv_in)
    projection_result = (
        jnp.dot(arrived, qkv_flat, preferred_element_type=jnp.float32)
        + low_rank_upward(low_rank_query_key_value, chosen_qkv_out)
        + qkv_bias
    )
    projection_result = projection_result.astype(jnp.bfloat16).reshape(
        seq_count, length, 3, local_heads, HEAD_DIM
    )
    queries = projection_result[:, :, 0]
    key_rows = projection_result[:, :, 1]
    values = projection_result[:, :, 2]
    attended_context, log_sums = attend(queries, key_rows, values, pieces, slopes)
    attended_context = attended_context.astype(jnp.bfloat16).reshape(full_rows, local_width)
    rank_ctx = low_rank_down(attended_context, chosen_out_in)
    ctx_term = low_rank_upward(rank_ctx, chosen_out_out)
    row_block = attended_context
    side_path = lax.psum_scatter(
        (jnp.dot(row_block, output_weight, preferred_element_type=jnp.float32) + ctx_term).astype(
            jnp.bfloat16
        ),
        "tensor",
        scatter_dimension=0,
        tiled=True,
    ).astype(jnp.float32)
    middle = inputs + (side_path + output_bias_vector)
    normed_mid_local, scaled_second, inverse_second = layer_norm(
        middle, norm_gains[1], norm_shifts[1]
    )
    normalized_middle = lax.all_gather(
        normed_mid_local.astype(jnp.bfloat16), "tensor", axis=0, tiled=True
    )
    rank_upper = low_rank_down(normalized_middle, chosen_up_in)
    gate_input_rows = (
        jnp.dot(normalized_middle, up_weight, preferred_element_type=jnp.float32)
        + low_rank_upward(rank_upper, chosen_up_out)
        + b_up
    )
    hidden_value, hidden_slope = gelu_parts(gate_input_rows)
    hidden_rows = hidden_value.astype(jnp.bfloat16)
    rank_lower = low_rank_down(hidden_rows, chosen_down_in)
    lower_term = low_rank_upward(rank_lower, chosen_down_out)
    row_block = hidden_rows
    mlp_part = lax.psum_scatter(
        (jnp.dot(row_block, down_weight, preferred_element_type=jnp.float32) + lower_term).astype(
            jnp.bfloat16
        ),
        "tensor",
        scatter_dimension=0,
        tiled=True,
    ).astype(jnp.float32)
    result = (middle + (mlp_part + down_bias_vector)).astype(jnp.bfloat16)
    grad_out = lax.all_gather(cotangent, "tensor", axis=0, tiled=True)
    grad_rank_lower = low_rank_down(grad_out, chosen_down_out)
    table_down_out = rank_grad(rank_lower, grad_out)
    table_down_in = rank_grad(grad_rank_lower, hidden_rows)
    grad_hidden = dot_transposed(grad_out, down_weight) + low_rank_upward(
        grad_rank_lower, chosen_down_in
    )
    grad_gate = (grad_hidden * hidden_slope).astype(jnp.bfloat16)
    grad_rank_upper = low_rank_down(grad_gate, chosen_up_out)
    table_up_out = rank_grad(rank_upper, grad_gate)
    table_up_in = rank_grad(grad_rank_upper, normalized_middle)
    upper_back = low_rank_upward(grad_rank_upper, chosen_up_in)
    row_block = grad_gate
    grad_mid_norm = lax.psum_scatter(
        (dot_transposed(row_block, up_weight) + upper_back).astype(jnp.bfloat16),
        "tensor",
        scatter_dimension=0,
        tiled=True,
    ).astype(jnp.float32)
    grad_middle = cotangent.astype(jnp.float32) + norm_back(
        grad_mid_norm, scaled_second, inverse_second, norm_gains[1]
    )
    grad_mid_low = lax.all_gather(grad_middle.astype(jnp.bfloat16), "tensor", axis=0, tiled=True)
    grad_rank_ctx = low_rank_down(grad_mid_low, chosen_out_out)
    table_out_out = rank_grad(rank_ctx, grad_mid_low)
    table_out_in = rank_grad(grad_rank_ctx, attended_context)
    grad_context = dot_transposed(grad_mid_low, output_weight) + low_rank_upward(
        grad_rank_ctx, chosen_out_in
    )
    grad_context = grad_context.astype(jnp.bfloat16).reshape(
        seq_count, length, local_heads, HEAD_DIM
    )
    grad_queries, grad_keys, grad_values = attend_back(
        queries, key_rows, values, pieces, slopes, log_sums, grad_context
    )
    grad_proj = (
        jnp.stack([grad_queries, grad_keys, grad_values], 2)
        .astype(jnp.bfloat16)
        .reshape(full_rows, 3 * local_width)
    )
    grad_rank_qkv = low_rank_down(grad_proj, chosen_qkv_out)
    table_qkv_out = rank_grad(low_rank_query_key_value, grad_proj)
    table_qkv_in = rank_grad(grad_rank_qkv, arrived)
    first_back = low_rank_upward(grad_rank_qkv, chosen_qkv_in)
    row_block = grad_proj
    grad_first = lax.psum_scatter(
        (dot_transposed(row_block, qkv_flat) + first_back).astype(jnp.bfloat16),
        "tensor",
        scatter_dimension=0,
        tiled=True,
    ).astype(jnp.float32)
    grad_tokens = (
        grad_middle + norm_back(grad_first, scaled_first, inverse_first, norm_gains[0])
    ).astype(jnp.bfloat16)
    shared = lax.psum(
        (
            to_tables(table_qkv_in, indicator_matrix[:, 0]),
            to_tables(table_out_out, indicator_matrix[:, 1]),
            to_tables(table_up_in, indicator_matrix[:, 2]),
            to_tables(table_down_out, indicator_matrix[:, 3]),
        ),
        ("dp", "tensor"),
    )
    owned_sums = (
        lax.psum(
            to_tables(table_qkv_out, indicator_matrix[:, 0])
            .reshape(qkv_out.shape)
            .astype(jnp.bfloat16),
            "dp",
        ).astype(jnp.float32),
        lax.psum(to_tables(table_out_in, indicator_matrix[:, 1]).astype(jnp.bfloat16), "dp").astype(
            jnp.float32
        ),
        lax.psum(to_tables(table_up_out, indicator_matrix[:, 2]).astype(jnp.bfloat16), "dp").astype(
            jnp.float32
        ),
        lax.psum(
            to_tables(table_down_in, indicator_matrix[:, 3]).astype(jnp.bfloat16), "dp"
        ).astype(jnp.float32),
    )
    return (
        result,
        grad_tokens,
        shared[0],
        owned_sums[0],
        owned_sums[1],
        shared[1],
        shared[2],
        owned_sums[2],
        owned_sums[3],
        shared[3],
    )


def solution(mesh):
    placed = (
        P(("dp", "tensor"), None),
        P(("dp", "tensor"), None),
        P(),
        P(),
        P(None, None, "tensor"),
        P(None, "tensor"),
        P("tensor", None),
        P(),
        P(None, "tensor"),
        P("tensor"),
        P("tensor", None),
        P(),
        P(),
        P(None, None, None, "tensor"),
        P(None, None, "tensor"),
        P(),
        P(),
        P(None, None, "tensor"),
        P(None, None, "tensor"),
        P(),
        P("dp", None),
        P("dp", None),
    )
    return jax.shard_map(
        body,
        mesh=mesh,
        in_specs=placed,
        out_specs=(
            P(("dp", "tensor"), None),
            P(("dp", "tensor"), None),
            P(),
            P(None, None, None, "tensor"),
            P(None, None, "tensor"),
            P(),
            P(),
            P(None, None, "tensor"),
            P(None, None, "tensor"),
            P(),
        ),
        check_vma=False,
    )
```

profile of v0, /device:TPU:0, one launch (start us, length us, event | category | flops | bytes accessed | tf_op | source)
XLA Modules:
  0.0 1041.3 jit_solution(12768031125403590012)
XLA Ops:
  17.7 9.0 copy.45
  38.1 60.4 %all-gather.5.cloned.1.call-done = bf16[1024,2048]{1,0:T(8,128)(2,1)} async-done(((bf16[256,2048]{1,0:T(8,128)(2,1)}), bf16[1024,2048]{1,0:T(8,128)(2,1)}) %all-gather.5.cloned.1.call-update) | async-done | bytes 4194320 | tf_op jit(solution)/shard_map/all_gather | solution.py:216
  102.0 8.8 fusion.112
  110.9 4.5 add_convert_fusion.4
  115.4 6.2 reshape.957
  121.6 4.2 fusion.104
  130.3 4.5 fusion.110
  151.7 5.6 add_convert_fusion.3
  158.2 74.7 %reduce-scatter.5.cloned.1.call-done = bf16[256,2048]{1,0:T(8,128)(2,1)} async-done(((bf16[1024,2048]{1,0:T(8,128)(2,1)}), bf16[256,2048]{1,0:T(8,128)(2,1)}) %reduce-scatter.5.cloned.1.call-update) | async-done | bytes 1048592 | tf_op jit(solution)/shard_map/reduce_scatter | solution.py:234
  245.7 70.1 %all-gather.9.cloned.1.call-done = bf16[1024,2048]{1,0:T(8,128)(2,1)} async-done(((bf16[256,2048]{1,0:T(8,128)(2,1)}), bf16[1024,2048]{1,0:T(8,128)(2,1)}) %all-gather.9.cloned.1.call-update) | async-done | bytes 4194320 | tf_op jit(solution)/shard_map/all_gather | solution.py:269
  315.8 4.2 fusion.74
  320.0 13.4 %fusion.115 = f32[1024,2048]{1,0:T(8,128)} fusion(bf16[1024,2048]{1,0:T(8,128)(2,1)S(1)} %copy-done.14, bf16[2048,2048]{1,0:T(8,128)(2,1)} %param.32), kind=kOutput, calls=%fused_computation.205 | convolution fusion | flops 8589934592 | bytes 20971520 | tf_op jit(solution)/shard_map/dot_general | solution.py:43
  333.4 63.8 %all-gather.7.cloned.1.call-done = bf16[1024,2048]{1,0:T(8,128)(2,1)} async-done(((bf16[256,2048]{1,0:T(8,128)(2,1)}), bf16[1024,2048]{1,0:T(8,128)(2,1)}) %all-gather.7.cloned.1.call-update) | async-done | bytes 4194320 | tf_op jit(solution)/shard_map/all_gather | solution.py:246
  400.8 13.3 %fusion.113 = f32[1024,2048]{1,0:T(8,128)} fusion(bf16[1024,2048]{1,0:T(8,128)(2,1)S(1)} %copy-done.9, bf16[2048,2048]{1,0:T(8,128)(2,1)} %param.30), kind=kOutput, calls=%fused_computation.203 | convolution fusion | flops 8589934592 | bytes 20971520 | tf_op jit(solution)/shard_map/dot_general | solution.py:251
  414.1 10.2 multiply_convert_fusion.2
  424.3 11.1 %fusion.6 = bf16[1024,2048]{1,0:T(8,128)(2,1)S(1)} fusion(f32[1024,2048]{1,0:T(8,128)S(1)} %get-tuple-element.55, f32[1024,2048]{1,0:T(8,128)} %fusion.115, f32[16,1024]{1,0:T(8,128)S(1)} %copy-done.49, bf16[1,16,2048]{2,0,1:T(2,128)(2,1)S(1)} %copy-done.45), kind=kOutput, calls=%fused_computation.8 | convolution fusion | flops 444596224 | bytes 21102592 | tf_op jit(solution)/shard_map/glr,grm->glm/dot_general | solution.py:61
  436.7 8.8 fusion.116
  445.5 5.3 add_convert_fusion.1
  454.8 11.9 %fusion.114 = f32[1024,2048]{1,0:T(8,128)S(1)} fusion(bf16[1024,2048]{1,0:T(8,128)(2,1)S(1)} %copy-done.13, bf16[2048,2048]{1,0:T(8,128)(2,1)} %param.32), kind=kOutput, calls=%fused_computation.204 | convolution fusion | flops 8589934592 | bytes 20971520 | tf_op jit(solution)/shard_map/dot_general | solution.py:261
  466.7 5.5 add_convert_fusion.2
  472.3 54.0 %reduce-scatter.9.cloned.1.call-done = bf16[256,2048]{1,0:T(8,128)(2,1)} async-done(((bf16[1024,2048]{1,0:T(8,128)(2,1)}), bf16[256,2048]{1,0:T(8,128)(2,1)}) %reduce-scatter.9.cloned.1.call-update) | async-done | bytes 1048592 | tf_op jit(solution)/shard_map/reduce_scatter | solution.py:282
  528.7 77.0 %reduce-scatter.7.cloned.1.call-done = bf16[256,2048]{1,0:T(8,128)(2,1)} async-done(((bf16[1024,2048]{1,0:T(8,128)(2,1)}), bf16[256,2048]{1,0:T(8,128)(2,1)}) %reduce-scatter.7.cloned.1.call-update) | async-done | bytes 1048592 | tf_op jit(solution)/shard_map/reduce_scatter | solution.py:260
  605.7 5.7 fusion.103
  614.5 4.1 fusion.123
  626.6 66.4 %all-gather.11.cloned.1.call-done = bf16[1024,2048]{1,0:T(8,128)(2,1)} async-done(((bf16[256,2048]{1,0:T(8,128)(2,1)}), bf16[1024,2048]{1,0:T(8,128)(2,1)}) %all-gather.11.cloned.1.call-update) | async-done | bytes 4194320 | tf_op jit(solution)/shard_map/all_gather | solution.py:291
  716.5 3.9 add_bitcast_fusion
  728.4 9.5 fusion.118
  742.0 7.7 add_convert_fusion
  750.5 4.1 fusion.120
  758.7 38.8 %all-reduce.7.cloned.1.call-done = (bf16[8,16,3,512]{3,1,2,0:T(8,128)(2,1)}, bf16[8,16,512]{2,1,0:T(8,128)(2,1)}, bf16[8,16,2048]{2,1,0:T(8,128)(2,1)}, bf16[8,16,2048]{2,1,0:T(8,128)(2,1)}) async-done(((bf16[8,16,3,512]{3,1,2,0:T(8,128)(2,1)}, bf16[8,16,512]{2,1,0:T(8,128)(2,1)}, bf16[8,16,2048]{2,1,0:T(8,128)(2,1)}, bf16[8,16,2048]{2,1,0:T(8,128)(2,1)}), (bf16[8,16,3,512]{3,1,2,0:T(8,128)(2,1)}, ...) | async-done | bytes 1572880 | tf_op jit(solution)/shard_map/psum | solution.py:333
  805.4 70.6 %reduce-scatter.11.cloned.1.call-done = bf16[256,2048]{1,0:T(8,128)(2,1)} async-done(((bf16[1024,2048]{1,0:T(8,128)(2,1)}), bf16[256,2048]{1,0:T(8,128)(2,1)}) %reduce-scatter.11.cloned.1.call-update) | async-done | bytes 1048592 | tf_op jit(solution)/shard_map/reduce_scatter | solution.py:314
  881.7 145.7 %all-reduce.5.cloned.1.call-done = (f32[8,16,2048]{2,1,0:T(8,128)}, f32[8,16,2048]{2,1,0:T(8,128)}, f32[8,16,2048]{2,1,0:T(8,128)}, f32[8,16,2048]{2,1,0:T(8,128)}) async-done(((f32[8,16,2048]{2,1,0:T(8,128)}, f32[8,16,2048]{2,1,0:T(8,128)}, f32[8,16,2048]{2,1,0:T(8,128)}, f32[8,16,2048]{2,1,0:T(8,128)}), (f32[8,16,2048]{2,1,0:T(8,128)}, f32[8,16,2048]{2,1,0:T(8,128)}, f32[8,16,2048]{2,1,0:T(8,128)}, ...) | async-done | bytes 4194320 | tf_op jit(solution)/shard_map/psum | solution.py:323
  (296 shorter events, 141.1 us)
Async XLA Ops:
  7.2 142.1 %copy-start = (bf16[512,2048]{1,0:T(8,128)(2,1)S(1)}, bf16[512,2048]{1,0:T(8,128)(2,1)}, u32[]{:S(2)}) copy-start(bf16[512,2048]{1,0:T(8,128)(2,1)} %param.28) | copy-start | bytes 6291460
  7.2 91.3 %all-gather.5.cloned.1.call-start = ((), (), s32[]{:S(2)}) async-start(), calls=%async_computation.4 | async-start | bytes 5242880 | tf_op jit(solution)/shard_map/all_gather | solution.py:216
  8.9 17.9 %copy-start.64 = (f32[256]{0:T(256)}, f32[256]{0:T(256)S(1)}, u32[]{:S(2)}) copy-start(f32[256]{0:T(256)S(1)} %broadcast_multiply_fusion.9) | copy-start | bytes 3076
  10.5 16.2 %copy-start.66 = (f32[256]{0:T(256)}, f32[256]{0:T(256)S(1)}, u32[]{:S(2)}) copy-start(f32[256]{0:T(256)S(1)} %add_rsqrt_fusion.1) | copy-start | bytes 3076
  11.4 15.4 %copy-start.52 = (f32[1,2048]{1,0:T(1,128)}, f32[1,2048]{1,0:T(1,128)S(1)}, u32[]{:S(2)}) copy-start(f32[1,2048]{1,0:T(1,128)S(1)} %get-tuple-element.28) | copy-start | bytes 24580
  14.9 218.0 %reduce-scatter.5.cloned.1.call-start = ((), (), s32[]{:S(2)}) async-start(), calls=%async_computation.5 | async-start | bytes 5242880 | tf_op jit(solution)/shard_map/reduce_scatter | solution.py:234
  17.7 13.9 %copy-start.54 = (bf16[8,16,512]{2,1,0:T(8,128)(2,1)S(1)}, bf16[8,16,512]{2,1,0:T(8,128)(2,1)}, u32[]{:S(2)}) copy-start(bf16[8,16,512]{2,1,0:T(8,128)(2,1)} %param.36) | copy-start | bytes 393220
  17.7 14.4 %copy-start.38 = (bf16[8,16,2048]{2,1,0:T(8,128)(2,1)S(1)}, bf16[8,16,2048]{2,1,0:T(8,128)(2,1)}, u32[]{:S(2)}) copy-start(bf16[8,16,2048]{2,1,0:T(8,128)(2,1)} %param.37) | copy-start | bytes 1572868
  31.6 206.5 %copy-start.55 = (bf16[1,4,8]{2,1,0:T(4,128)(2,1)}, bf16[1,4,8]{2,1,0:T(4,128)(2,1)S(1)}, u32[]{:S(2)}) copy-start(bf16[1,4,8]{2,1,0:T(4,128)(2,1)S(1)} %get-tuple-element.47) | copy-start | bytes 196
  31.9 117.1 %copy-start.56 = (bf16[1,16,512]{2,0,1:T(2,128)(2,1)}, bf16[1,16,512]{2,0,1:T(2,128)(2,1)S(1)}, u32[]{:S(2)}) copy-start(bf16[1,16,512]{2,0,1:T(2,128)(2,1)S(1)} %fusion.65) | copy-start | bytes 49156
  32.1 78.7 %copy-start.40 = (bf16[1,16,1536]{2,0,1:T(2,128)(2,1)}, bf16[1,16,1536]{2,0,1:T(2,128)(2,1)S(1)}, u32[]{:S(2)}) copy-start(bf16[1,16,1536]{2,0,1:T(2,128)(2,1)S(1)} %fusion.89) | copy-start | bytes 147460
  34.1 67.9 %copy-start.34 = (bf16[1,16,2048]{2,0,1:T(2,128)(2,1)}, bf16[1,16,2048]{2,0,1:T(2,128)(2,1)S(1)}, u32[]{:S(2)}) copy-start(bf16[1,16,2048]{2,0,1:T(2,128)(2,1)S(1)} %fusion.59) | copy-start | bytes 196612
  125.8 14.7 %copy-start.16 = (bf16[1,1024,1,4,128]{4,3,2,1,0:T(4,128)(2,1)}, bf16[1,1024,1,4,128]{4,3,2,1,0:T(4,128)(2,1)S(1)}, u32[]{:S(2)}) copy-start(bf16[1,1024,1,4,128]{4,3,2,1,0:T(4,128)(2,1)S(1)} %get-tuple-element.25) | copy-start | bytes 3145732
  157.3 75.5 %copy-start.3 = (bf16[256,2048]{1,0:T(8,128)(2,1)S(1)}, bf16[256,2048]{1,0:T(8,128)(2,1)}, u32[]{:S(2)}) copy-start(bf16[256,2048]{1,0:T(8,128)(2,1)} %param.22) | copy-start | bytes 3145732
  157.3 75.5 %copy-start.51 = (f32[2048]{0:T(1024)S(1)}, f32[2048]{0:T(1024)}, u32[]{:S(2)}) copy-start(f32[2048]{0:T(1024)} %param.29) | copy-start | bytes 24580
  157.4 158.4 %all-gather.9.cloned.1.call-start = ((), (), s32[]{:S(2)}) async-start(), calls=%async_computation.8 | async-start | bytes 5242880 | tf_op jit(solution)/shard_map/all_gather | solution.py:269
  158.1 239.1 %all-gather.7.cloned.1.call-start = ((), (), s32[]{:S(2)}) async-start(), calls=%async_computation.6 | async-start | bytes 5242880 | tf_op jit(solution)/shard_map/all_gather | solution.py:246
  238.1 288.2 %reduce-scatter.9.cloned.1.call-start = ((), (), s32[]{:S(2)}) async-start(), calls=%async_computation.9 | async-start | bytes 5242880 | tf_op jit(solution)/shard_map/reduce_scatter | solution.py:282
  245.7 151.5 %copy-start.36 = (bf16[1,16,2048]{2,0,1:T(2,128)(2,1)}, bf16[1,16,2048]{2,0,1:T(2,128)(2,1)S(1)}, u32[]{:S(2)}) copy-start(bf16[1,16,2048]{2,0,1:T(2,128)(2,1)S(1)} %fusion.55) | copy-start | bytes 196612
  414.1 22.5 %slice-start.6 = ((s8[8388608]{0:T(1024)(128)(4,1)}), s8[4194304]{0:T(1024)(128)(4,1)S(1)}, s32[]{:S(2)}) async-start(s8[8388608]{0:T(1024)(128)(4,1)} %bitcast.268), calls=%async_computation.20 | async-start | bytes 8388608
  450.9 154.9 %reduce-scatter.7.cloned.1.call-start = ((), (), s32[]{:S(2)}) async-start(), calls=%async_computation.7 | async-start | bytes 5242880 | tf_op jit(solution)/shard_map/reduce_scatter | solution.py:260
  472.2 54.1 %copy-start.63 = (f32[256]{0:T(256)S(1)}, f32[256]{0:T(256)}, u32[]{:S(2)}) copy-start(f32[256]{0:T(256)} %copy-done.62) | copy-start | bytes 3076
  472.2 54.1 %copy-start.69 = (f32[256]{0:T(256)S(1)}, f32[256]{0:T(256)}, u32[]{:S(2)}) copy-start(f32[256]{0:T(256)} %copy-done.68) | copy-start | bytes 3076
  472.2 133.5 %copy-start.70 = (f32[2048]{0:T(1024)S(1)}, f32[2048]{0:T(1024)}, u32[]{:S(2)}) copy-start(f32[2048]{0:T(1024)} %param.33) | copy-start | bytes 24580
  472.2 220.7 %all-gather.11.cloned.1.call-start = ((), (), s32[]{:S(2)}) async-start(), calls=%async_computation.10 | async-start | bytes 5242880 | tf_op jit(solution)/shard_map/all_gather | solution.py:291
  528.7 85.8 %copy-start.50 = (f32[16,1024]{1,0:T(8,128)S(1)}, f32[16,1024]{1,0:T(8,128)}, u32[]{:S(2)}) copy-start(f32[16,1024]{1,0:T(8,128)} %fusion.74) | copy-start | bytes 196612
  611.5 186.1 %all-reduce.7.cloned.1.call-start = ((), (), s32[]{:S(2)}) async-start(), calls=%async_computation.13 | async-start | bytes 3145728 | tf_op jit(solution)/shard_map/psum | solution.py:333
  739.5 136.5 %reduce-scatter.11.cloned.1.call-start = ((), (), s32[]{:S(2)}) async-start(), calls=%async_computation.11 | async-start | bytes 5242880 | tf_op jit(solution)/shard_map/reduce_scatter | solution.py:314
  749.7 277.6 %all-reduce.5.cloned.1.call-start = ((), (), s32[]{:S(2)}) async-start(), calls=%async_computation.12 | async-start | bytes 8388608 | tf_op jit(solution)/shard_map/psum | solution.py:323
  758.7 117.4 %copy-start.53 = (f32[1,2048]{1,0:T(1,128)S(1)}, f32[1,2048]{1,0:T(1,128)}, u32[]{:S(2)}) copy-start(f32[1,2048]{1,0:T(1,128)} %copy-done.52) | copy-start | bytes 24580
  758.7 117.4 %copy-start.65 = (f32[256]{0:T(256)S(1)}, f32[256]{0:T(256)}, u32[]{:S(2)}) copy-start(f32[256]{0:T(256)} %copy-done.64) | copy-start | bytes 3076
  758.7 117.4 %copy-start.67 = (f32[256]{0:T(256)S(1)}, f32[256]{0:T(256)}, u32[]{:S(2)}) copy-start(f32[256]{0:T(256)} %copy-done.66) | copy-start | bytes 3076
  (67 other events, 367.0 us)
Sparse Core Ops, SparseCore 0:
  15.0 83.4 all-gather.4
  157.5 75.2 reduce-scatter.4
  234.5 81.2 all-gather.8
  317.9 79.2 all-gather.6
  451.0 75.2 reduce-scatter.8
  528.5 77.2 reduce-scatter.6
  611.6 81.2 all-gather.10
  739.7 57.8 all-reduce.6
  799.9 76.1 reduce-scatter.10
  883.9 143.3 all-reduce.4
where the time goes:
time: 1050 us; the launch traced here: 1040 us
  waiting for transfers between devices  722 us (69%)
  matrix products  203 us (19%)
  other arithmetic  58.5 us (6%)
  local copies, waits for them, and re-layouts  39.8 us (4%)
  between operations  17 us (2%)
    psum x1, waiting for transfers between devices, body(): lax.psum((to_tables(table_qkv_in, indicator_matrix[:, 0]), to_tables(tabl...  146 us
    reduce_scatter x1, waiting for transfers between devices, body(): lax.psum_scatter((jnp.dot(row_block, down_weight, preferred_element_type=...  77 us
    reduce_scatter x1, waiting for transfers between devices, body(): lax.psum_scatter((jnp.dot(row_block, output_weight, preferred_element_typ...  74.7 us
    reduce_scatter x1, waiting for transfers between devices, body(): lax.psum_scatter((dot_transposed(row_block, qkv_flat) + first_back).astyp...  70.6 us
    all_gather x1, waiting for transfers between devices, body(): grad_out = lax.all_gather(cotangent, 'tensor', axis=0, tiled=True)  70.1 us
    all_gather x1, waiting for transfers between devices, body(): lax.all_gather(grad_middle.astype(jnp.bfloat16), 'tensor', axis=0, tiled=...  66.4 us
    all_gather x1, waiting for transfers between devices, body(): lax.all_gather(normed_mid_local.astype(jnp.bfloat16), 'tensor', axis=0, t...  63.8 us
    all_gather x1, waiting for transfers between devices, body(): arrived = lax.all_gather(sent_in, 'tensor', axis=0, tiled=True)  60.4 us
  transfers between devices with their start and end apart: 10, of which 10 were waited for; matrix products, arithmetic and copies ran while one was open for 12% of the time, Pallas kernels for 0%

commit v1 on v0

--- a/solution.py
+++ b/solution.py
@@ -12,6 +12,18 @@
 GELU_K = 0.044715
 NEGATIVE = -1e30
 EXACT_MODE = lax.Precision.HIGHEST
+
+
+def gather_by_bits(x, axis, dim):
+    ways, here = (lax.axis_size(axis), lax.axis_index(axis))
+    grown, reach = (x, 1)
+    while reach < ways:
+        theirs = lax.ppermute(grown, axis, [(d, d ^ reach) for d in range(ways)])
+        mine_first = jnp.concatenate([grown, theirs], axis=dim)
+        theirs_first = jnp.concatenate([theirs, grown], axis=dim)
+        grown = jnp.where(here & reach == 0, mine_first, theirs_first)
+        reach = 2 * reach
+    return grown
 
 
 def layer_norm(values, gain_row, shift_row):
@@ -288,7 +300,7 @@
     grad_middle = cotangent.astype(jnp.float32) + norm_back(
         grad_mid_norm, scaled_second, inverse_second, norm_gains[1]
     )
-    grad_mid_low = lax.all_gather(grad_middle.astype(jnp.bfloat16), "tensor", axis=0, tiled=True)
+    grad_mid_low = gather_by_bits(grad_middle.astype(jnp.bfloat16), "tensor", 0)
     grad_rank_ctx = low_rank_down(grad_mid_low, chosen_out_out)
     table_out_out = rank_grad(rank_ctx, grad_mid_low)
     table_out_in = rank_grad(grad_rank_ctx, attended_context)

time: 1050 us -> 1090 us (1.038)
  waiting for transfers between devices: 722 us -> 761 us
    ppermute x0 -> x2, waiting for transfers between devices: none -> 104 us  [gather_by_bits(): theirs = lax.ppermute(grown, axis, [(d, d ^ reach) for d in range(ways)])]
    all_gather x1 -> x0, waiting for transfers between devices: 66.4 us -> none  [body(): lax.all_gather(grad_middle.astype(jnp.bfloat16), 'tensor', axis=0, tiled=...]
    unnamed x185 -> x197, local copies, waits for them, and re-layouts: 26.3 us -> 26.4 us
  transfers between devices with their start and end apart: 10 -> 11, of which waited for: 10 -> 11; matrix products, arithmetic and copies ran while one was open for 12% -> 11% of each run, Pallas kernels for 0% -> 0%
where the time goes in v1:
time: 1090 us; the launch traced here: 1080 us
  waiting for transfers between devices  761 us (70%)
  matrix products  200 us (18%)
  other arithmetic  59.5 us (5%)
  local copies, waits for them, and re-layouts  40 us (4%)
  between operations  16.5 us (2%)
    psum x1, waiting for transfers between devices, body(): lax.psum((to_tables(table_qkv_in, indicator_matrix[:, 0]), to_tables(tabl...  146 us
    ppermute x2, waiting for transfers between devices, gather_by_bits(): theirs = lax.ppermute(grown, axis, [(d, d ^ reach) for d in range(ways)])  104 us
    reduce_scatter x1, waiting for transfers between devices, body(): lax.psum_scatter((jnp.dot(row_block, down_weight, preferred_element_type=...  77 us
    reduce_scatter x1, waiting for transfers between devices, body(): lax.psum_scatter((jnp.dot(row_block, output_weight, preferred_element_typ...  74.7 us
    all_gather x1, waiting for transfers between devices, body(): grad_out = lax.all_gather(cotangent, 'tensor', axis=0, tiled=True)  70.8 us
    reduce_scatter x1, waiting for transfers between devices, body(): lax.psum_scatter((dot_transposed(row_block, qkv_flat) + first_back).astyp...  70.6 us
    all_gather x1, waiting for transfers between devices, body(): lax.all_gather(normed_mid_local.astype(jnp.bfloat16), 'tensor', axis=0, t...  63.7 us
    all_gather x1, waiting for transfers between devices, body(): arrived = lax.all_gather(sent_in, 'tensor', axis=0, tiled=True)  60.2 us
  transfers between devices with their start and end apart: 11, of which 11 were waited for; matrix products, arithmetic and copies ran while one was open for 11% of the time, Pallas kernels for 0%

profile of v1, /device:TPU:0, one launch (start us, length us, event | category | flops | bytes accessed | tf_op | source)
XLA Modules:
  0.0 1082.3 jit_solution(13715077041143899116)
XLA Ops:
  17.7 9.0 copy.45
  38.3 60.2 %all-gather.4.cloned.1.call-done = bf16[1024,2048]{1,0:T(8,128)(2,1)} async-done(((bf16[256,2048]{1,0:T(8,128)(2,1)}), bf16[1024,2048]{1,0:T(8,128)(2,1)}) %all-gather.4.cloned.1.call-update) | async-done | bytes 4194320 | tf_op jit(solution)/shard_map/all_gather | solution.py:228
  102.0 8.8 fusion.114
  110.9 4.5 add_convert_fusion.4
  115.4 6.2 reshape.972
  121.6 4.2 fusion.106
  130.4 4.5 fusion.112
  151.8 5.6 add_convert_fusion.3
  158.2 74.7 %reduce-scatter.5.cloned.1.call-done = bf16[256,2048]{1,0:T(8,128)(2,1)} async-done(((bf16[1024,2048]{1,0:T(8,128)(2,1)}), bf16[256,2048]{1,0:T(8,128)(2,1)}) %reduce-scatter.5.cloned.1.call-update) | async-done | bytes 1048592 | tf_op jit(solution)/shard_map/reduce_scatter | solution.py:246
  245.0 70.8 %all-gather.8.cloned.1.call-done = bf16[1024,2048]{1,0:T(8,128)(2,1)} async-done(((bf16[256,2048]{1,0:T(8,128)(2,1)}), bf16[1024,2048]{1,0:T(8,128)(2,1)}) %all-gather.8.cloned.1.call-update) | async-done | bytes 4194320 | tf_op jit(solution)/shard_map/all_gather | solution.py:281
  315.8 4.2 fusion.74
  320.0 13.5 %fusion.117 = f32[1024,2048]{1,0:T(8,128)} fusion(bf16[1024,2048]{1,0:T(8,128)(2,1)S(1)} %copy-done.13, bf16[2048,2048]{1,0:T(8,128)(2,1)} %param.32), kind=kOutput, calls=%fused_computation.209 | convolution fusion | flops 8589934592 | bytes 20971520 | tf_op jit(solution)/shard_map/dot_general | solution.py:55
  333.5 63.7 %all-gather.6.cloned.1.call-done = bf16[1024,2048]{1,0:T(8,128)(2,1)} async-done(((bf16[256,2048]{1,0:T(8,128)(2,1)}), bf16[1024,2048]{1,0:T(8,128)(2,1)}) %all-gather.6.cloned.1.call-update) | async-done | bytes 4194320 | tf_op jit(solution)/shard_map/all_gather | solution.py:258
  400.8 13.4 %fusion.115 = f32[1024,2048]{1,0:T(8,128)} fusion(bf16[1024,2048]{1,0:T(8,128)(2,1)S(1)} %copy-done.7, bf16[2048,2048]{1,0:T(8,128)(2,1)} %param.30), kind=kOutput, calls=%fused_computation.207 | convolution fusion | flops 8589934592 | bytes 20971520 | tf_op jit(solution)/shard_map/dot_general | solution.py:263
  414.2 10.2 multiply_convert_fusion.2
  424.3 11.4 %fusion.6 = bf16[1024,2048]{1,0:T(8,128)(2,1)S(1)} fusion(f32[1024,2048]{1,0:T(8,128)S(1)} %get-tuple-element.55, f32[1024,2048]{1,0:T(8,128)} %fusion.117, f32[16,1024]{1,0:T(8,128)S(1)} %copy-done.48, bf16[1,16,2048]{2,0,1:T(2,128)(2,1)S(1)} %fusion.51), kind=kOutput, calls=%fused_computation.8 | convolution fusion | flops 444596224 | bytes 21102592 | tf_op jit(solution)/shard_map/glr,grm->glm/dot_general | solution.py:73
  436.9 8.8 fusion.118
  445.8 5.3 add_convert_fusion.1
  455.8 11.5 %fusion.116 = f32[1024,2048]{1,0:T(8,128)S(1)} fusion(bf16[1024,2048]{1,0:T(8,128)(2,1)S(1)} %copy-done.11, bf16[2048,2048]{1,0:T(8,128)(2,1)} %param.32), kind=kOutput, calls=%fused_computation.208 | convolution fusion | flops 8589934592 | bytes 20971520 | tf_op jit(solution)/shard_map/dot_general | solution.py:273
  467.3 5.5 add_convert_fusion.2
  473.1 53.5 %reduce-scatter.9.cloned.1.call-done = bf16[256,2048]{1,0:T(8,128)(2,1)} async-done(((bf16[1024,2048]{1,0:T(8,128)(2,1)}), bf16[256,2048]{1,0:T(8,128)(2,1)}) %reduce-scatter.9.cloned.1.call-update) | async-done | bytes 1048592 | tf_op jit(solution)/shard_map/reduce_scatter | solution.py:294
  529.0 77.0 %reduce-scatter.7.cloned.1.call-done = bf16[256,2048]{1,0:T(8,128)(2,1)} async-done(((bf16[1024,2048]{1,0:T(8,128)(2,1)}), bf16[256,2048]{1,0:T(8,128)(2,1)}) %reduce-scatter.7.cloned.1.call-update) | async-done | bytes 1048592 | tf_op jit(solution)/shard_map/reduce_scatter | solution.py:272
  606.0 5.8 fusion.105
  613.4 23.6 %collective-permute-done = bf16[256,2048]{1,0:T(8,128)(2,1)} collective-permute-done((bf16[256,2048]{1,0:T(8,128)(2,1)}, bf16[256,2048]{1,0:T(8,128)(2,1)}, u32[]{:S(2)}, u32[]{:S(2)}) %collective-permute-start) | collective-permute-done | bytes 1048608 | tf_op jit(solution)/shard_map/ppermute | solution.py:21
  653.2 80.0 %collective-permute-done.1 = bf16[512,2048]{1,0:T(8,128)(2,1)S(1)} collective-permute-done((bf16[512,2048]{1,0:T(8,128)(2,1)S(1)}, bf16[512,2048]{1,0:T(8,128)(2,1)S(1)}, u32[]{:S(2)}, u32[]{:S(2)}) %collective-permute-start.1) | collective-permute-done | bytes 2097184 | tf_op jit(solution)/shard_map/ppermute | solution.py:21
  736.7 5.6 add_convert_fusion.5
  768.5 9.3 fusion.119
  781.9 7.5 add_convert_fusion
  789.5 4.1 fusion.120
  799.0 40.1 %all-reduce.7.cloned.1.call-done = (bf16[8,16,3,512]{3,1,2,0:T(8,128)(2,1)}, bf16[8,16,512]{2,1,0:T(8,128)(2,1)}, bf16[8,16,2048]{2,1,0:T(8,128)(2,1)}, bf16[8,16,2048]{2,1,0:T(8,128)(2,1)}) async-done(((bf16[8,16,3,512]{3,1,2,0:T(8,128)(2,1)}, bf16[8,16,512]{2,1,0:T(8,128)(2,1)}, bf16[8,16,2048]{2,1,0:T(8,128)(2,1)}, bf16[8,16,2048]{2,1,0:T(8,128)(2,1)}), (bf16[8,16,3,512]{3,1,2,0:T(8,128)(2,1)}, ...) | async-done | bytes 1572880 | tf_op jit(solution)/shard_map/psum | solution.py:345
  846.9 70.6 %reduce-scatter.11.cloned.1.call-done = bf16[256,2048]{1,0:T(8,128)(2,1)} async-done(((bf16[1024,2048]{1,0:T(8,128)(2,1)}), bf16[256,2048]{1,0:T(8,128)(2,1)}) %reduce-scatter.11.cloned.1.call-update) | async-done | bytes 1048592 | tf_op jit(solution)/shard_map/reduce_scatter | solution.py:326
  923.1 145.9 %all-reduce.5.cloned.1.call-done = (f32[8,16,2048]{2,1,0:T(8,128)}, f32[8,16,2048]{2,1,0:T(8,128)}, f32[8,16,2048]{2,1,0:T(8,128)}, f32[8,16,2048]{2,1,0:T(8,128)}) async-done(((f32[8,16,2048]{2,1,0:T(8,128)}, f32[8,16,2048]{2,1,0:T(8,128)}, f32[8,16,2048]{2,1,0:T(8,128)}, f32[8,16,2048]{2,1,0:T(8,128)}), (f32[8,16,2048]{2,1,0:T(8,128)}, f32[8,16,2048]{2,1,0:T(8,128)}, f32[8,16,2048]{2,1,0:T(8,128)}, ...) | async-done | bytes 4194320 | tf_op jit(solution)/shard_map/psum | solution.py:335
  (310 shorter events, 146.8 us)
Async XLA Ops:
  7.2 142.1 %copy-start = (bf16[512,2048]{1,0:T(8,128)(2,1)S(1)}, bf16[512,2048]{1,0:T(8,128)(2,1)}, u32[]{:S(2)}) copy-start(bf16[512,2048]{1,0:T(8,128)(2,1)} %param.28) | copy-start | bytes 6291460
  7.2 91.3 %all-gather.4.cloned.1.call-start = ((), (), s32[]{:S(2)}) async-start(), calls=%async_computation.4 | async-start | bytes 5242880 | tf_op jit(solution)/shard_map/all_gather | solution.py:228
  14.9 218.0 %reduce-scatter.5.cloned.1.call-start = ((), (), s32[]{:S(2)}) async-start(), calls=%async_computation.5 | async-start | bytes 5242880 | tf_op jit(solution)/shard_map/reduce_scatter | solution.py:246
  31.8 210.0 %copy-start.54 = (bf16[1,4,8]{2,1,0:T(4,128)(2,1)}, bf16[1,4,8]{2,1,0:T(4,128)(2,1)S(1)}, u32[]{:S(2)}) copy-start(bf16[1,4,8]{2,1,0:T(4,128)(2,1)S(1)} %get-tuple-element.47) | copy-start | bytes 196
  32.0 117.1 %copy-start.55 = (bf16[1,16,512]{2,0,1:T(2,128)(2,1)}, bf16[1,16,512]{2,0,1:T(2,128)(2,1)S(1)}, u32[]{:S(2)}) copy-start(bf16[1,16,512]{2,0,1:T(2,128)(2,1)S(1)} %fusion.65) | copy-start | bytes 49156
  32.3 78.6 %copy-start.38 = (bf16[1,16,1536]{2,0,1:T(2,128)(2,1)}, bf16[1,16,1536]{2,0,1:T(2,128)(2,1)S(1)}, u32[]{:S(2)}) copy-start(bf16[1,16,1536]{2,0,1:T(2,128)(2,1)S(1)} %fusion.90) | copy-start | bytes 147460
  32.7 119.0 %copy-start.43 = (bf16[1,16,2048]{2,0,1:T(2,128)(2,1)}, bf16[1,16,2048]{2,0,1:T(2,128)(2,1)S(1)}, u32[]{:S(2)}) copy-start(bf16[1,16,2048]{2,0,1:T(2,128)(2,1)S(1)} %fusion.57) | copy-start | bytes 196612
  157.4 75.5 %copy-start.50 = (f32[2048]{0:T(1024)S(1)}, f32[2048]{0:T(1024)}, u32[]{:S(2)}) copy-start(f32[2048]{0:T(1024)} %param.29) | copy-start | bytes 24580
  157.4 158.4 %all-gather.8.cloned.1.call-start = ((), (), s32[]{:S(2)}) async-start(), calls=%async_computation.8 | async-start | bytes 5242880 | tf_op jit(solution)/shard_map/all_gather | solution.py:281
  158.1 239.1 %all-gather.6.cloned.1.call-start = ((), (), s32[]{:S(2)}) async-start(), calls=%async_computation.6 | async-start | bytes 5242880 | tf_op jit(solution)/shard_map/all_gather | solution.py:258
  238.1 288.5 %reduce-scatter.9.cloned.1.call-start = ((), (), s32[]{:S(2)}) async-start(), calls=%async_computation.9 | async-start | bytes 5242880 | tf_op jit(solution)/shard_map/reduce_scatter | solution.py:294
  243.4 181.0 %copy-start.45 = (bf16[1,16,2048]{2,0,1:T(2,128)(2,1)}, bf16[1,16,2048]{2,0,1:T(2,128)(2,1)S(1)}, u32[]{:S(2)}) copy-start(bf16[1,16,2048]{2,0,1:T(2,128)(2,1)S(1)} %fusion.51) | copy-start | bytes 196612
  451.1 154.9 %reduce-scatter.7.cloned.1.call-start = ((), (), s32[]{:S(2)}) async-start(), calls=%async_computation.7 | async-start | bytes 5242880 | tf_op jit(solution)/shard_map/reduce_scatter | solution.py:272
  472.8 133.2 %copy-start.76 = (f32[2048]{0:T(1024)S(1)}, f32[2048]{0:T(1024)}, u32[]{:S(2)}) copy-start(f32[2048]{0:T(1024)} %param.33) | copy-start | bytes 24580
  472.9 366.2 %all-reduce.7.cloned.1.call-start = ((), (), s32[]{:S(2)}) async-start(), calls=%async_computation.12 | async-start | bytes 3145728 | tf_op jit(solution)/shard_map/psum | solution.py:345
  529.0 84.3 %copy-start.75 = (pred[1,4,8]{2,1,0:T(4,128)(4,1)S(1)}, pred[1,4,8]{2,1,0:T(4,128)(4,1)}, u32[]{:S(2)}) copy-start(pred[1,4,8]{2,1,0:T(4,128)(4,1)} %get-tuple-element.46) | copy-start | bytes 100
  529.0 84.3 %copy-start.60 = (f32[4,512]{1,0:T(4,128)S(1)}, f32[4,512]{1,0:T(4,128)}, u32[]{:S(2)}) copy-start(f32[4,512]{1,0:T(4,128)} %copy-done.59) | copy-start | bytes 24580
  529.0 84.3 %copy-start.62 = (f32[4,512]{1,0:T(4,128)S(1)}, f32[4,512]{1,0:T(4,128)}, u32[]{:S(2)}) copy-start(f32[4,512]{1,0:T(4,128)} %copy-done.61) | copy-start | bytes 24580
  529.0 84.3 %copy-start.64 = (f32[4,512]{1,0:T(4,128)S(1)}, f32[4,512]{1,0:T(4,128)}, u32[]{:S(2)}) copy-start(f32[4,512]{1,0:T(4,128)} %copy-done.63) | copy-start | bytes 24580
  529.0 84.3 %copy-start.66 = (f32[4,512]{1,0:T(4,128)S(1)}, f32[4,512]{1,0:T(4,128)}, u32[]{:S(2)}) copy-start(f32[4,512]{1,0:T(4,128)} %copy-done.65) | copy-start | bytes 24580
  611.7 25.3 %collective-permute-start = (bf16[256,2048]{1,0:T(8,128)(2,1)}, bf16[256,2048]{1,0:T(8,128)(2,1)}, u32[]{:S(2)}, u32[]{:S(2)}) collective-permute-start(bf16[256,2048]{1,0:T(8,128)(2,1)} %get-tuple-element.22), channel_id=1, source_target_pairs={{0,1},{1,0},{2,3},{3,2},{4,5},{5,4},{6,7},{7,6},{8,9},{9,8},{10,11... | collective-permute-start | bytes 3145736 | tf_op jit(solution)/shard_map/ppermute | solution.py:21
  640.4 96.2 %copy-start.26 = (bf16[512,2048]{1,0:T(8,128)(2,1)}, bf16[512,2048]{1,0:T(8,128)(2,1)S(1)}, u32[]{:S(2)}) copy-start(bf16[512,2048]{1,0:T(8,128)(2,1)S(1)} %maximum_select_fusion.1) | copy-start | bytes 6291460
  640.4 92.8 %collective-permute-start.1 = (bf16[512,2048]{1,0:T(8,128)(2,1)S(1)}, bf16[512,2048]{1,0:T(8,128)(2,1)S(1)}, u32[]{:S(2)}, u32[]{:S(2)}) collective-permute-start(bf16[512,2048]{1,0:T(8,128)(2,1)S(1)} %maximum_select_fusion.1), channel_id=1, source_target_pairs={{0,2},{1,3},{2,0},{3,1},{4,6},{5,7},{6,4},{7,5},{8,10},{9,11},{10,... | collective-permute-start | bytes 6291464 | tf_op jit(solution)/shard_map/ppermute | solution.py:21
  648.7 84.5 %copy-start.44 = (bf16[1,16,2048]{2,0,1:T(2,128)(2,1)S(1)}, bf16[1,16,2048]{2,0,1:T(2,128)(2,1)}, u32[]{:S(2)}) copy-start(bf16[1,16,2048]{2,0,1:T(2,128)(2,1)} %copy-done.43) | copy-start | bytes 196612
  653.2 81.2 %copy-start.84 = (bf16[4,128,512]{2,1,0:T(8,128)(2,1)S(1)}, bf16[4,128,512]{2,1,0:T(8,128)(2,1)}, u32[]{:S(2)}) copy-start(bf16[4,128,512]{2,1,0:T(8,128)(2,1)} %copy-done.83) | copy-start | bytes 1572868
  653.2 81.2 %copy-start.86 = (bf16[4,128,512]{2,1,0:T(8,128)(2,1)S(1)}, bf16[4,128,512]{2,1,0:T(8,128)(2,1)}, u32[]{:S(2)}) copy-start(bf16[4,128,512]{2,1,0:T(8,128)(2,1)} %copy-done.85) | copy-start | bytes 1572868
  653.2 82.2 %copy-start.56 = (bf16[1,16,512]{2,0,1:T(2,128)(2,1)S(1)}, bf16[1,16,512]{2,0,1:T(2,128)(2,1)}, u32[]{:S(2)}) copy-start(bf16[1,16,512]{2,0,1:T(2,128)(2,1)} %copy-done.55) | copy-start | bytes 49156
  779.4 138.1 %reduce-scatter.11.cloned.1.call-start = ((), (), s32[]{:S(2)}) async-start(), calls=%async_computation.10 | async-start | bytes 5242880 | tf_op jit(solution)/shard_map/reduce_scatter | solution.py:326
  789.4 279.6 %all-reduce.5.cloned.1.call-start = ((), (), s32[]{:S(2)}) async-start(), calls=%async_computation.11 | async-start | bytes 8388608 | tf_op jit(solution)/shard_map/psum | solution.py:335
  798.9 118.6 %copy-start.52 = (f32[1,2048]{1,0:T(1,128)S(1)}, f32[1,2048]{1,0:T(1,128)}, u32[]{:S(2)}) copy-start(f32[1,2048]{1,0:T(1,128)} %copy-done.51) | copy-start | bytes 24580
  798.9 118.6 %copy-start.70 = (f32[256]{0:T(256)S(1)}, f32[256]{0:T(256)}, u32[]{:S(2)}) copy-start(f32[256]{0:T(256)} %copy-done.69) | copy-start | bytes 3076
  799.0 118.6 %copy-start.72 = (f32[256]{0:T(256)S(1)}, f32[256]{0:T(256)}, u32[]{:S(2)}) copy-start(f32[256]{0:T(256)} %copy-done.71) | copy-start | bytes 3076
  (74 other events, 816.0 us)
Sparse Core Ops, SparseCore 0:
  15.0 83.4 all-gather.3
  157.5 75.2 reduce-scatter.4
  234.5 81.2 all-gather.7
  317.9 79.2 all-gather.5
  451.2 75.2 reduce-scatter.8
  528.7 77.2 reduce-scatter.6
  779.5 59.4 all-reduce.6
  841.3 76.1 reduce-scatter.10
  925.5 143.4 all-reduce.4
